TPU v7x, 512 devices: a whole 4x8x8 slice. The times are simulated.
512 devices in a mesh: seq: 32 (over x, y), chan: 16 (over z, core).
Axes of the slice: x: 4, y: 8, z: 8, core: 2. Of those that a mesh axis runs over, the one named last changes fastest.
Arguments:
- tokens: bfloat16 [1536, 16384], P('chan', 'seq'), may hold values from -6 to 6
- gate_weight: bfloat16 [1536, 1536], P('chan'), may hold values from -0.15625 to 0.15625
- value_weight: bfloat16 [1536, 1536], P('chan'), may hold values from -0.15625 to 0.15625
- first_factor: bfloat16 [64, 256, 256], P('seq'), may hold values from -0.375 to 0.375
- second_factor: bfloat16 [256, 64, 64], P('seq'), may hold values from -0.75 to 0.75
- down_latent: bfloat16 [1536, 128], P('chan'), may hold values from -0.15625 to 0.15625
- up_latent: bfloat16 [1536, 128], P('chan'), may hold values from -0.5 to 0.5
- doc_lengths: int32 [64], replicated, may hold values from 1 to 8704, 16384 in all
- cotangent: bfloat16 [1536, 16384], P('chan', 'seq'), may hold values from -6 to 6
Outputs:
- hidden: bfloat16 [1536, 16384], P('chan', 'seq')
- d_gate_weight: float32 [1536, 1536], P('chan')
- d_value_weight: float32 [1536, 1536], P('chan')
- d_first: float32 [64, 256, 256], P('seq', 'chan')
- d_second: float32 [256, 64, 64], P('seq', 'chan')
- d_down: float32 [1536, 128], P('chan')
- d_up: float32 [1536, 128], P('chan')
Inputs may be any that keep to these rules, and one draw needn't show every extreme that they name: `doc_lengths`: the documents' lengths sum to 16384; the longest is exactly 8704 tokens.
All inputs are finite; a program needn't handle non-finite values.
Results may differ from a plain program's by a relative error of at most 0.0058.
Values may be sent and summed in bfloat16 or wider, within the bound.
No kernel may reach another device: no remote copies, remote signals or barrier semaphores. Data moves between devices by JAX's collectives and lax.ppermute only.
A program may use at most 64 MiB of HBM per device.

v0:
```python
import jax
import jax.numpy as jnp
from jax import lax
from jax.sharding import PartitionSpec as P
from jax.experimental import pallas as pl
from jax.experimental.pallas import tpu as pltpu


HIGHEST = lax.Precision.HIGHEST


def seq_exchange(x):
    return lax.all_to_all(x, "seq", 0, 0, tiled=True)


def tiled_exchange(x):
    n, width = x.shape
    unit = 8 * 128
    padded = -(-width // unit) * unit
    x = jnp.pad(x, ((0, 0), (0, padded - width))).reshape(n, padded // 128, 128)
    return seq_exchange(x).reshape(n, padded)[:, :width]


def split_hi_lo(x):
    hi = lax.reduce_precision(x, exponent_bits=8, mantissa_bits=7)
    lo = x - hi
    return jnp.concatenate([hi.astype(jnp.bfloat16), lo.astype(jnp.bfloat16)], axis=-1)


def join_hi_lo(x):
    n = x.shape[-1] // 2
    return x[..., :n].astype(jnp.float32) + x[..., n:].astype(jnp.float32)


def epilogue_kernel(fac_ref, xdoc_ref, scale_ref, first_ref, second_ref, down_ref):
    blocks, kp, width = first_ref.shape
    k_here, m_part, nb2 = second_ref.shape
    lanes = fac_ref.shape[1]
    rows_first = blocks * kp * width // lanes
    per_row = width // lanes
    for i in range(blocks):
        for h in range(per_row):
            first_ref[i, :, pl.ds(h * lanes, lanes)] = fac_ref[pl.ds(i * kp * per_row + h, kp, stride=per_row), :]
    rows_second = k_here * m_part * nb2 // lanes
    per_lane_row = lanes // nb2
    for k in range(k_here):
        for m in range(m_part):
            r = rows_first + (k * m_part + m) // per_lane_row
            off = (m % per_lane_row) * nb2
            second_ref[k, pl.ds(m, 1), :] = fac_ref[pl.ds(r, 1), pl.ds(off, nb2)]
    g0 = rows_first + rows_second
    g = fac_ref[pl.ds(g0, fac_ref.shape[0] - g0), :]
    dp = lax.reduce_precision(g * scale_ref[...], exponent_bits=8, mantissa_bits=7)
    down_ref[...] = jnp.dot(xdoc_ref[...], dp, precision=HIGHEST, preferred_element_type=jnp.float32)


def epilogue(fac, xdoc, scale_col, first_shape, second_shape):
    f32 = jnp.float32
    vmem = pl.BlockSpec(memory_space=pltpu.VMEM)
    return pl.pallas_call(
        epilogue_kernel,
        out_shape=(jax.ShapeDtypeStruct(first_shape, f32), jax.ShapeDtypeStruct(second_shape, f32),
                   jax.ShapeDtypeStruct((xdoc.shape[0], fac.shape[1]), f32)),
        in_specs=[vmem] * 3,
        out_specs=[vmem] * 3,
        cost_estimate=pl.CostEstimate(
            flops=2 * xdoc.shape[0] * xdoc.shape[1] * fac.shape[1] * 6,
            bytes_accessed=4 * (2 * fac.size + xdoc.size + xdoc.shape[0] * fac.shape[1]),
            transcendentals=0,
        ),
    )(fac, xdoc, scale_col)


def body(
    tokens,
    gate_weight,
    value_weight,
    first_factor,
    second_factor,
    down_latent,
    up_latent,
    doc_lengths,
    cotangent,
):
    n_seq = lax.axis_size("seq")
    n_chan = lax.axis_size("chan")
    chan_rows, tok_cols = tokens.shape
    blocks_here, block_width, _ = first_factor.shape
    k_here, n_blk2, _ = second_factor.shape
    lat = down_latent.shape[1]
    n_doc = doc_lengths.shape[0]
    docs_here = n_doc // n_seq
    me = lax.axis_index("seq")

    packed = jnp.concatenate([tokens, down_latent], axis=1)
    gathered_all = lax.all_gather(packed, "chan", axis=0, tiled=True)
    gathered = gathered_all[:, :tok_cols]
    down_full = gathered_all[:, tok_cols:]

    doc_ends = jnp.cumsum(doc_lengths)
    doc_begins = doc_ends - doc_lengths
    position = me * tok_cols + jnp.arange(tok_cols, dtype=jnp.int32)
    member = (
        (position[None, :] >= doc_begins[:, None]) & (position[None, :] < doc_ends[:, None])
    ).astype(jnp.float32)
    len_scale = lax.rsqrt(doc_lengths.astype(jnp.float32))

    gate_pre = jnp.dot(gate_weight, gathered, preferred_element_type=jnp.float32)
    value_bf = jnp.dot(value_weight, gathered, preferred_element_type=jnp.float32).astype(
        jnp.bfloat16
    )
    latent = jnp.einsum("ct,cl->lt", gathered, down_full, preferred_element_type=jnp.float32)
    doc_lat_part = jnp.einsum("dt,lt->dl", member, latent, precision=HIGHEST)
    xdoc_part = jnp.einsum(
        "ct,dt->cd", tokens, member.astype(jnp.bfloat16), preferred_element_type=jnp.float32
    )

    blocked = value_bf.reshape(chan_rows, blocks_here, block_width)
    inner_mix = jnp.einsum(
        "ikj,cij->ikc", first_factor, blocked, preferred_element_type=jnp.float32
    ).astype(jnp.bfloat16)

    sig = jax.nn.sigmoid(gate_pre)
    act = gate_pre * sig
    upstream = cotangent.astype(jnp.float32)
    d_mixed = upstream * act
    d_mixed_bf = d_mixed.astype(jnp.bfloat16)
    per_doc_part = jnp.einsum("ct,dt->cd", d_mixed, member, precision=HIGHEST)

    inner_send = inner_mix.reshape(blocks_here, n_seq, k_here, chan_rows).transpose(1, 0, 2, 3)
    d_send = d_mixed_bf.reshape(chan_rows, blocks_here, n_seq, k_here).transpose(2, 1, 3, 0)
    mix_send = jnp.concatenate([inner_send, d_send], axis=3).reshape(n_seq, -1)
    n_mix = mix_send.shape[1]

    small_send = jnp.concatenate(
        [
            doc_lat_part.reshape(n_seq, docs_here * lat),
            per_doc_part.reshape(chan_rows, n_seq, docs_here)
            .transpose(1, 0, 2)
            .reshape(n_seq, chan_rows * docs_here),
            xdoc_part.reshape(chan_rows, n_seq, docs_here)
            .transpose(1, 0, 2)
            .reshape(n_seq, chan_rows * docs_here),
        ],
        axis=1,
    )
    recv2 = tiled_exchange(jnp.concatenate([mix_send, split_hi_lo(small_send)], axis=1))
    mix2 = recv2[:, :n_mix].reshape(n_seq, blocks_here, k_here, 2 * chan_rows)
    columns = mix2[..., :chan_rows].reshape(n_seq * blocks_here, k_here, chan_rows)
    d_outer = mix2[..., chan_rows:].reshape(n_seq * blocks_here, k_here, chan_rows)
    small_red = jnp.sum(join_hi_lo(recv2[:, n_mix:]), axis=0)
    n_a = docs_here * lat
    n_b = chan_rows * docs_here
    scale_here = lax.dynamic_slice(len_scale, (me * docs_here,), (docs_here,))
    pooled_here = small_red[:n_a].reshape(docs_here, lat) * scale_here[:, None]
    per_doc_here = small_red[n_a : n_a + n_b].reshape(chan_rows, docs_here)
    xdoc_here = small_red[n_a + n_b :].reshape(chan_rows, docs_here)

    up_float = up_latent.astype(jnp.float32)
    g_part = jnp.einsum("cd,cl->dl", per_doc_here, up_float, precision=HIGHEST)

    outer_mix = jnp.einsum(
        "kmi,ikc->mkc", second_factor, columns, preferred_element_type=jnp.float32
    ).astype(jnp.bfloat16)
    d_inner = jnp.einsum(
        "kmi,mkc->ikc", second_factor, d_outer, preferred_element_type=jnp.float32
    ).astype(jnp.bfloat16)
    d_second_part = jnp.einsum(
        "mkc,ikc->kmi", d_outer, columns, preferred_element_type=jnp.float32
    )

    outer_send = outer_mix.reshape(n_seq, blocks_here, k_here, chan_rows)
    dinner_send = d_inner.reshape(n_seq, blocks_here, k_here, chan_rows)
    piece = jnp.concatenate(
        [
            pooled_here.reshape(n_a),
            per_doc_here.reshape(n_b),
            xdoc_here.reshape(n_b),
            g_part.reshape(n_a),
        ]
    )
    piece_b = jnp.broadcast_to(split_hi_lo(piece)[None, :], (n_seq, 2 * piece.shape[0]))
    send3 = jnp.concatenate(
        [jnp.concatenate([outer_send, dinner_send], axis=3).reshape(n_seq, -1), piece_b], axis=1
    )
    recv3_all = tiled_exchange(send3)
    recv3 = recv3_all[:, :n_mix].reshape(n_seq, blocks_here, k_here, 2 * chan_rows)
    gath3 = join_hi_lo(recv3_all[:, n_mix:])
    outer_tok = (
        recv3[..., :chan_rows].transpose(3, 1, 0, 2).reshape(chan_rows, tok_cols).astype(jnp.float32)
    )
    d_rows = recv3[..., chan_rows:].transpose(1, 0, 2, 3).reshape(
        blocks_here, n_seq * k_here, chan_rows
    )
    pooled = gath3[:, :n_a].reshape(n_doc, lat)
    per_doc = (
        gath3[:, n_a : n_a + n_b].reshape(n_seq, chan_rows, docs_here).transpose(1, 0, 2)
    ).reshape(chan_rows, n_doc)
    xdoc = (
        gath3[:, n_a + n_b : n_a + 2 * n_b].reshape(n_seq, chan_rows, docs_here).transpose(1, 0, 2)
    ).reshape(chan_rows, n_doc)
    g_gath = gath3[:, n_a + 2 * n_b :].reshape(1, n_doc * lat)

    spread = jnp.einsum("dl,cl->cd", pooled, up_float, precision=HIGHEST)
    summary = jnp.dot(spread, member, precision=HIGHEST)
    mixed = outer_tok + summary
    hidden = (act * mixed).astype(jnp.bfloat16)
    d_gate_bf = (upstream * mixed * sig * (1.0 + gate_pre * (1.0 - sig))).astype(jnp.bfloat16)

    d_value_bf = (
        jnp.einsum("ikj,ikc->cij", first_factor, d_rows, preferred_element_type=jnp.float32)
        .astype(jnp.bfloat16)
        .reshape(chan_rows, tok_cols)
    )
    d_first_part = jnp.einsum("ikc,cij->ikj", d_rows, blocked, preferred_element_type=jnp.float32)
    d_up = jnp.einsum("cd,dl->cl", per_doc, pooled, precision=HIGHEST)

    both_grads = jnp.concatenate([d_gate_bf, d_value_bf], axis=0)
    d_proj_part = jnp.einsum("ot,it->oi", both_grads, gathered, preferred_element_type=jnp.float32)
    rows_here = 2 * chan_rows // n_seq
    width = d_proj_part.shape[1]

    proj_send = d_proj_part.reshape(n_seq, rows_here, width).astype(jnp.bfloat16)
    proj_red = jnp.sum(seq_exchange(proj_send).astype(jnp.float32), axis=0)
    k_part = block_width // n_chan
    m_part = n_blk2 // n_chan
    first_send = (
        d_first_part.reshape(blocks_here, n_chan, k_part, block_width)
        .transpose(1, 0, 2, 3)
        .reshape(n_chan, -1)
    )
    second_send = (
        d_second_part.reshape(k_here, n_chan, m_part, n_blk2).transpose(1, 0, 2, 3).reshape(n_chan, -1)
    )
    g_send = jnp.broadcast_to(g_gath, (n_chan, n_doc * lat))
    fac_send = jnp.concatenate([first_send, second_send, g_send], axis=1)
    fac_red = lax.psum_scatter(fac_send.reshape(-1, 128), "chan", scatter_dimension=0, tiled=True)
    proj_bf = proj_red.astype(jnp.bfloat16)
    gath5 = seq_exchange(jnp.broadcast_to(proj_bf[None], (n_seq, rows_here, width)))
    d_first, d_second, d_down = epilogue(
        fac_red,
        xdoc,
        len_scale.reshape(n_doc, 1),
        (blocks_here, k_part, block_width),
        (k_here, m_part, n_blk2),
    )
    d_proj = gath5.reshape(2 * chan_rows, width).astype(jnp.float32)
    return (hidden, d_proj[:chan_rows], d_proj[chan_rows:], d_first, d_second, d_down, d_up)


def solution(mesh):
    in_specs = (
        P("chan", "seq"),
        P("chan", None),
        P("chan", None),
        P("seq", None, None),
        P("seq", None, None),
        P("chan", None),
        P("chan", None),
        P(),
        P("chan", "seq"),
    )
    out_specs = (
        P("chan", "seq"),
        P("chan", None),
        P("chan", None),
        P("seq", "chan", None),
        P("seq", "chan", None),
        P("chan", None),
        P("chan", None),
    )

    return jax.shard_map(body, mesh=mesh, in_specs=in_specs, out_specs=out_specs, check_vma=False)
```

profile of v0, /device:TPU:1, one launch (start us, length us, event | category | flops | bytes accessed | tf_op | source)
XLA Modules:
  0.0 194.3 jit_solution(8418558650380938522)
XLA Ops:
  7.2 1.6 pad_maximum_fusion.3
  8.9 0.7 copy.61
  9.9 0.7 sub.12
  10.5 1.1 fusion.31
  11.8 47.6 %all-gather.2.cloned.1.call-done = bf16[1536,640]{1,0:T(8,128)(2,1)} async-done(((bf16[96,640]{1,0:T(8,128)(2,1)}), bf16[1536,640]{1,0:T(8,128)(2,1)}) %all-gather.2.cloned.1.call-update) | async-done | bytes 1966096 | tf_op jit(solution)/shard_map/all_gather | solution.py:96
  59.4 1.9 convolution_convert_fusion.3
  61.3 0.2 fusion
  61.7 2.0 %fusion.3 = f32[128,512]{1,0:T(8,128)S(1)} fusion(bf16[1536,640]{1,0:T(8,128)(2,1)} %all-gather.2.cloned.1.call-done), kind=kOutput, calls=%fused_computation.13 | convolution fusion | flops 201326592 | bytes 2228224 | tf_op jit(solution)/shard_map/ct,cl->lt/dot_general | solution.py:112
  63.6 0.3 fusion.36
  63.9 1.8 fusion.22
  66.1 0.3 reshape.183
  66.4 0.3 fusion.21
  67.0 0.8 copy.97
  67.7 9.4 %all-to-all-start = ((bf16[32,40,128]{2,1,0:T(8,128)(2,1)}), bf16[32,40,128]{2,1,0:T(8,128)(2,1)S(1)}, u32[]{:S(2)}, u32[]{:S(2)}) async-start(bf16[32,40,128]{2,1,0:T(8,128)(2,1)} %bitcast.60), calls=%async_computation | async-start | bytes 655360 | tf_op jit(solution)/shard_map/all_to_all | solution.py:13
  77.3 10.5 %all-to-all-done = bf16[32,40,128]{2,1,0:T(8,128)(2,1)S(1)} async-done(((bf16[32,40,128]{2,1,0:T(8,128)(2,1)}), bf16[32,40,128]{2,1,0:T(8,128)(2,1)S(1)}, u32[]{:S(2)}, u32[]{:S(2)}) %all-to-all-start) | async-done | bytes 327712 | tf_op jit(solution)/shard_map/all_to_all | solution.py:13
  88.1 0.3 reshape.193
  89.1 0.2 convolution_convert_fusion.2
  89.6 0.3 reshape.198
  89.9 0.2 convolution_bitcast_fusion.1
  90.2 0.8 copy.99
  91.0 7.4 %all-to-all-start.1 = ((bf16[32,40,128]{2,1,0:T(8,128)(2,1)}), bf16[32,40,128]{2,1,0:T(8,128)(2,1)S(1)}, u32[]{:S(2)}, u32[]{:S(2)}) async-start(bf16[32,40,128]{2,1,0:T(8,128)(2,1)} %bitcast.65), calls=%async_computation.1 | async-start | bytes 655360 | tf_op jit(solution)/shard_map/all_to_all | solution.py:13
  98.4 0.2 fusion.43
  98.7 0.2 reshape.211
  98.9 9.5 %all-to-all-done.1 = bf16[32,40,128]{2,1,0:T(8,128)(2,1)S(1)} async-done(((bf16[32,40,128]{2,1,0:T(8,128)(2,1)}), bf16[32,40,128]{2,1,0:T(8,128)(2,1)S(1)}, u32[]{:S(2)}, u32[]{:S(2)}) %all-to-all-start.1) | async-done | bytes 327712 | tf_op jit(solution)/shard_map/all_to_all | solution.py:13
  108.4 1.0 copy.71
  109.6 0.2 copy.76
  109.8 0.2 fusion.1
  110.0 0.2 fusion.23
  110.2 0.2 copy.92
  110.8 0.2 fusion.42
  111.0 1.0 fusion.16
  112.0 2.1 %convolution_convert_fusion = bf16[192,1536]{1,0:T(8,128)(2,1)S(1)} fusion(bf16[1536,640]{1,0:T(8,128)(2,1)} %all-gather.2.cloned.1.call-done, bf16[96,512]{1,0:T(8,128)(2,1)S(1)} %bitcast.144, bf16[96,512]{1,0:T(8,128)(2,1)S(1)} %get-tuple-element.21), kind=kOutput, calls=%fused_computation | convolution fusion | flops 302678016 | bytes 2359296 | tf_op jit(solution)/shard_map/ot,it->oi/dot_general | solution.py:219
  114.1 1.1 convert_element_type.130
  115.2 7.3 %all-to-all-start.2 = ((bf16[32,6,1536]{2,1,0:T(8,128)(2,1)}), bf16[32,6,1536]{2,1,0:T(8,128)(2,1)S(1)}, u32[]{:S(2)}, u32[]{:S(2)}) async-start(bf16[32,6,1536]{2,1,0:T(8,128)(2,1)} %convert_element_type.130), calls=%async_computation.2 | async-start | bytes 1572864 | tf_op jit(solution)/shard_map/all_to_all | solution.py:13
  122.6 0.3 copy.100
  123.0 1.2 reshape.212
  124.2 17.0 %all-to-all-done.2 = bf16[32,6,1536]{2,1,0:T(8,128)(2,1)S(1)} async-done(((bf16[32,6,1536]{2,1,0:T(8,128)(2,1)}), bf16[32,6,1536]{2,1,0:T(8,128)(2,1)S(1)}, u32[]{:S(2)}, u32[]{:S(2)}) %all-to-all-start.2) | async-done | bytes 589856 | tf_op jit(solution)/shard_map/all_to_all | solution.py:13
  141.4 1.0 broadcast_in_dim.9
  142.3 8.3 %all-to-all-start.3 = ((bf16[32,6,1536]{2,1,0:T(8,128)(2,1)}), bf16[32,6,1536]{2,1,0:T(8,128)(2,1)S(1)}, u32[]{:S(2)}, u32[]{:S(2)}) async-start(bf16[32,6,1536]{2,1,0:T(8,128)(2,1)} %broadcast_in_dim.9), calls=%async_computation.3 | async-start | bytes 1572864 | tf_op jit(solution)/shard_map/all_to_all | solution.py:13
  150.7 0.7 copy.86.scale_ref
  151.6 0.7 copy.85.xdoc_ref
  152.3 0.9 fusion.44
  153.2 16.3 %all-to-all-done.3 = bf16[32,6,1536]{2,1,0:T(8,128)(2,1)S(1)} async-done(((bf16[32,6,1536]{2,1,0:T(8,128)(2,1)}), bf16[32,6,1536]{2,1,0:T(8,128)(2,1)S(1)}, u32[]{:S(2)}, u32[]{:S(2)}) %all-to-all-start.3) | async-done | bytes 589856 | tf_op jit(solution)/shard_map/all_to_all | solution.py:13
  169.5 0.2 fusion.38
  169.6 0.9 slice.120
  170.5 0.9 slice.118
  171.4 14.2 %reduce-scatter.2.cloned.1.call-done.fac_ref = f32[144,128]{1,0:T(8,128)} async-done(((f32[2304,128]{1,0:T(8,128)}), f32[144,128]{1,0:T(8,128)}) %reduce-scatter.2.cloned.1.call-update) | async-done | bytes 73744 | tf_op jit(solution)/shard_map/reduce_scatter | solution.py:237
  185.7 1.8 shard_map.144
  (70 shorter events, 3.7 us)
Async XLA Ops:
  7.2 56.8 %copy-start = (bf16[96,1536]{1,0:T(8,128)(2,1)S(1)}, bf16[96,1536]{1,0:T(8,128)(2,1)}, u32[]{:S(2)}) copy-start(bf16[96,1536]{1,0:T(8,128)(2,1)} %param.10) | copy-start | bytes 884740
  7.2 54.1 %copy-start.1 = (bf16[2,256,256]{2,1,0:T(8,128)(2,1)S(1)}, bf16[2,256,256]{2,1,0:T(8,128)(2,1)}, u32[]{:S(2)}) copy-start(bf16[2,256,256]{2,1,0:T(8,128)(2,1)} %param.12) | copy-start | bytes 786436
  7.2 52.2 %all-gather.2.cloned.1.call-start = ((), (), s32[]{:S(2)}) async-start(), calls=%async_computation.5 | async-start | bytes 2088960 | tf_op jit(solution)/shard_map/all_gather | solution.py:96
  61.3 2.6 %copy-start.5 = (bf16[96,512]{1,0:T(8,128)(2,1)S(1)}, bf16[96,512]{1,0:T(8,128)(2,1)}, u32[]{:S(2)}) copy-start(bf16[96,512]{1,0:T(8,128)(2,1)} %param.17) | copy-start | bytes 294916
  66.4 10.8 %copy-start.4 = (s32[64]{0:T(128)S(1)}, s32[64]{0:T(128)}, u32[]{:S(2)}) copy-start(s32[64]{0:T(128)} %param.16) | copy-start | bytes 772
  67.7 20.9 %copy-start.2 = (bf16[8,64,64]{2,1,0:T(8,128)(2,1)S(1)}, bf16[8,64,64]{2,1,0:T(8,128)(2,1)}, u32[]{:S(2)}) copy-start(bf16[8,64,64]{2,1,0:T(8,128)(2,1)} %param.13) | copy-start | bytes 196612
  67.7 20.0 %all-to-all-start = ((bf16[32,40,128]{2,1,0:T(8,128)(2,1)}), bf16[32,40,128]{2,1,0:T(8,128)(2,1)S(1)}, u32[]{:S(2)}, u32[]{:S(2)}) async-start(bf16[32,40,128]{2,1,0:T(8,128)(2,1)} %bitcast.60), calls=%async_computation | async-start | bytes 655360 | tf_op jit(solution)/shard_map/all_to_all | solution.py:13
  88.4 1.5 copy-start.3
  91.0 17.4 %all-to-all-start.1 = ((bf16[32,40,128]{2,1,0:T(8,128)(2,1)}), bf16[32,40,128]{2,1,0:T(8,128)(2,1)S(1)}, u32[]{:S(2)}, u32[]{:S(2)}) async-start(bf16[32,40,128]{2,1,0:T(8,128)(2,1)} %bitcast.65), calls=%async_computation.1 | async-start | bytes 655360 | tf_op jit(solution)/shard_map/all_to_all | solution.py:13
  115.2 26.0 %all-to-all-start.2 = ((bf16[32,6,1536]{2,1,0:T(8,128)(2,1)}), bf16[32,6,1536]{2,1,0:T(8,128)(2,1)S(1)}, u32[]{:S(2)}, u32[]{:S(2)}) async-start(bf16[32,6,1536]{2,1,0:T(8,128)(2,1)} %convert_element_type.130), calls=%async_computation.2 | async-start | bytes 1572864 | tf_op jit(solution)/shard_map/all_to_all | solution.py:13
  122.5 63.2 %reduce-scatter.2.cloned.1.call-start = ((), (), s32[]{:S(2)}) async-start(), calls=%async_computation.6 | async-start | bytes 1253376 | tf_op jit(solution)/shard_map/reduce_scatter | solution.py:237
  142.3 27.1 %all-to-all-start.3 = ((bf16[32,6,1536]{2,1,0:T(8,128)(2,1)}), bf16[32,6,1536]{2,1,0:T(8,128)(2,1)S(1)}, u32[]{:S(2)}, u32[]{:S(2)}) async-start(bf16[32,6,1536]{2,1,0:T(8,128)(2,1)} %broadcast_in_dim.9), calls=%async_computation.3 | async-start | bytes 1572864 | tf_op jit(solution)/shard_map/all_to_all | solution.py:13
Sparse Core Ops, SparseCore 0:
  10.7 48.6 all-gather.1
  126.1 59.5 reduce-scatter.1
where the time goes:
time: 197 us; the launch traced here: 194 us
  waiting for transfers between devices  115 us (58%)
  starting transfers between devices  32.5 us (16%)
  between operations  14.6 us (7%)
  local copies, waits for them, and re-layouts  14 us (7%)
  matrix products  12.9 us (7%)
  other arithmetic  3.41 us (2%)
    all_to_all x4, waiting for transfers between devices, seq_exchange(): return lax.all_to_all(x, 'seq', 0, 0, tiled=True)  53.2 us
    all_gather x1, waiting for transfers between devices, body(): gathered_all = lax.all_gather(packed, 'chan', axis=0, tiled=True)  47.6 us
    all_to_all x4, starting transfers between devices, seq_exchange(): return lax.all_to_all(x, 'seq', 0, 0, tiled=True)  32.4 us
    reduce_scatter x1, waiting for transfers between devices, body(): lax.psum_scatter(fac_send.reshape(-1, 128), 'chan', scatter_dimension=0,...  14.2 us
  transfers between devices with their start and end apart: 6, of which 6 were waited for; matrix products, arithmetic and copies ran while one was open for 6% of the time, Pallas kernels for 0%

commit v1 on v0

--- a/solution.py
+++ b/solution.py
@@ -11,14 +11,6 @@
 
 def seq_exchange(x):
     return lax.all_to_all(x, "seq", 0, 0, tiled=True)
-
-
-def tiled_exchange(x):
-    n, width = x.shape
-    unit = 8 * 128
-    padded = -(-width // unit) * unit
-    x = jnp.pad(x, ((0, 0), (0, padded - width))).reshape(n, padded // 128, 128)
-    return seq_exchange(x).reshape(n, padded)[:, :width]
 
 
 def split_hi_lo(x):
@@ -71,6 +63,27 @@
     )(fac, xdoc, scale_col)
 
 
+def proj_kernel(in_ref, gate_ref, val_ref):
+    n, rows, _ = in_ref.shape
+    half = n // 2
+    for s in range(n):
+        dst = gate_ref if s < half else val_ref
+        dst[pl.ds((s % half) * rows, rows), :] = in_ref[s].astype(jnp.float32)
+
+
+def proj_unpack(gath):
+    n, rows, width = gath.shape
+    shape = jax.ShapeDtypeStruct((n // 2 * rows, width), jnp.float32)
+    vmem = pl.BlockSpec(memory_space=pltpu.VMEM)
+    return pl.pallas_call(
+        proj_kernel,
+        out_shape=(shape, shape),
+        in_specs=[vmem],
+        out_specs=[vmem, vmem],
+        cost_estimate=pl.CostEstimate(flops=0, bytes_accessed=gath.size * 6, transcendentals=0),
+    )(gath)
+
+
 def body(
     tokens,
     gate_weight,
@@ -144,7 +157,7 @@
         ],
         axis=1,
     )
-    recv2 = tiled_exchange(jnp.concatenate([mix_send, split_hi_lo(small_send)], axis=1))
+    recv2 = seq_exchange(jnp.concatenate([mix_send, split_hi_lo(small_send)], axis=1))
     mix2 = recv2[:, :n_mix].reshape(n_seq, blocks_here, k_here, 2 * chan_rows)
     columns = mix2[..., :chan_rows].reshape(n_seq * blocks_here, k_here, chan_rows)
     d_outer = mix2[..., chan_rows:].reshape(n_seq * blocks_here, k_here, chan_rows)
@@ -183,7 +196,7 @@
     send3 = jnp.concatenate(
         [jnp.concatenate([outer_send, dinner_send], axis=3).reshape(n_seq, -1), piece_b], axis=1
     )
-    recv3_all = tiled_exchange(send3)
+    recv3_all = seq_exchange(send3)
     recv3 = recv3_all[:, :n_mix].reshape(n_seq, blocks_here, k_here, 2 * chan_rows)
     gath3 = join_hi_lo(recv3_all[:, n_mix:])
     outer_tok = (
@@ -244,8 +257,8 @@
         (blocks_here, k_part, block_width),
         (k_here, m_part, n_blk2),
     )
-    d_proj = gath5.reshape(2 * chan_rows, width).astype(jnp.float32)
-    return (hidden, d_proj[:chan_rows], d_proj[chan_rows:], d_first, d_second, d_down, d_up)
+    d_gate_w, d_value_w = proj_unpack(gath5)
+    return (hidden, d_gate_w, d_value_w, d_first, d_second, d_down, d_up)
 
 
 def solution(mesh):

time: 197 us -> 183 us (0.929)
  the two profiles are of different devices: /device:TPU:1 before, /device:TPU:8 now
where the time goes in v1:
time: 183 us; the launch traced here: 182 us
  waiting for transfers between devices  90.9 us (50%)
  blocking collectives  26.4 us (14%)
  starting transfers between devices  19.5 us (11%)
  between operations  14.6 us (8%)
  local copies, waits for them, and re-layouts  12 us (7%)
  matrix products  9.73 us (5%)
  other arithmetic  5.1 us (3%)
  Pallas kernels  4.01 us (2%)
    all_gather x1, waiting for transfers between devices, body(): gathered_all = lax.all_gather(packed, 'chan', axis=0, tiled=True)  46.3 us
    all_to_all x3, waiting for transfers between devices, seq_exchange(): return lax.all_to_all(x, 'seq', 0, 0, tiled=True)  44.6 us
    all_to_all x1, blocking collectives, seq_exchange(): return lax.all_to_all(x, 'seq', 0, 0, tiled=True)  26.4 us
    all_to_all x3, starting transfers between devices, seq_exchange(): return lax.all_to_all(x, 'seq', 0, 0, tiled=True)  19.4 us
  transfers between devices with their start and end apart: 5, of which 4 were waited for; matrix products, arithmetic and copies ran while one was open for 6% of the time, Pallas kernels for 1%

profile of v1, /device:TPU:8, one launch (start us, length us, event | category | flops | bytes accessed | tf_op | source)
XLA Modules:
  0.0 182.3 jit_solution(4465653238998908376)
XLA Ops:
  7.2 1.6 pad_maximum_fusion.2
  8.9 0.7 copy.92
  9.9 0.7 sub.12
  10.5 1.1 fusion.27
  11.8 46.3 %all-gather.2.cloned.1.call-done = bf16[1536,640]{1,0:T(8,128)(2,1)} async-done(((bf16[96,640]{1,0:T(8,128)(2,1)}), bf16[1536,640]{1,0:T(8,128)(2,1)}) %all-gather.2.cloned.1.call-update) | async-done | bytes 1966096 | tf_op jit(solution)/shard_map/all_gather | solution.py:109
  58.1 2.0 %convolution_convert_fusion.3 = bf16[512,96]{0,1:T(8,128)(2,1)S(1)} fusion(bf16[96,1536]{1,0:T(8,128)(2,1)} %param.11, bf16[1536,640]{1,0:T(8,128)(2,1)} %all-gather.2.cloned.1.call-done), kind=kOutput, calls=%fused_computation.6 | convolution fusion | flops 151044096 | bytes 1966080 | tf_op jit(solution)/shard_map/dot_general | solution.py:122
  60.1 0.2 fusion
  60.5 0.4 fusion.3
  60.9 0.3 fusion.32
  61.2 0.4 fusion.16
  62.0 0.3 reshape.171
  62.2 0.3 fusion.15
  62.9 0.5 broadcast.26
  63.4 0.8 reduce.2
  64.2 0.8 reshape.206
  65.0 9.9 %all-to-all-start = ((bf16[32,2,2176]{2,1,0:T(2,128)(2,1)}), bf16[32,2,2176]{2,1,0:T(2,128)(2,1)S(1)}, u32[]{:S(2)}, u32[]{:S(2)}) async-start(bf16[32,2,2176]{2,1,0:T(2,128)(2,1)} %reshape.206), calls=%async_computation | async-start | bytes 557056 | tf_op jit(solution)/shard_map/all_to_all | solution.py:13
  74.9 12.9 %all-to-all-done = bf16[32,2,2176]{2,1,0:T(2,128)(2,1)S(1)} async-done(((bf16[32,2,2176]{2,1,0:T(2,128)(2,1)}), bf16[32,2,2176]{2,1,0:T(2,128)(2,1)S(1)}, u32[]{:S(2)}, u32[]{:S(2)}) %all-to-all-start) | async-done | bytes 278560 | tf_op jit(solution)/shard_map/all_to_all | solution.py:13
  87.8 0.2 reshape.207
  88.4 0.3 reshape.179
  89.4 0.2 convolution_convert_fusion.2
  89.9 0.3 reshape.184
  90.2 0.2 convolution_bitcast_fusion.1
  90.5 0.8 reduce.3
  91.3 0.8 reshape.208
  92.1 4.6 %all-to-all-start.1 = ((bf16[32,2,2432]{2,1,0:T(2,128)(2,1)}), bf16[32,2,2432]{2,1,0:T(2,128)(2,1)S(1)}, u32[]{:S(2)}, u32[]{:S(2)}) async-start(bf16[32,2,2432]{2,1,0:T(2,128)(2,1)} %reshape.208), calls=%async_computation.1 | async-start | bytes 622592 | tf_op jit(solution)/shard_map/all_to_all | solution.py:13
  96.8 0.2 fusion.37
  97.0 0.2 reshape.195
  97.3 12.4 %all-to-all-done.1 = bf16[32,2,2432]{2,1,0:T(2,128)(2,1)S(1)} async-done(((bf16[32,2,2432]{2,1,0:T(2,128)(2,1)}), bf16[32,2,2432]{2,1,0:T(2,128)(2,1)S(1)}, u32[]{:S(2)}, u32[]{:S(2)}) %all-to-all-start.1) | async-done | bytes 311328 | tf_op jit(solution)/shard_map/all_to_all | solution.py:13
  109.7 0.3 reshape.209
  110.1 0.3 reshape.188
  110.5 0.2 fusion.1
  110.7 0.2 fusion.17
  111.0 0.2 fusion.36
  111.4 0.3 copy.126
  111.8 1.2 reshape.196
  113.0 2.1 %fusion.10 = (bf16[96,512]{1,0:T(8,128)(2,1)S(1)}, bf16[96,512]{1,0:T(8,128)(2,1)}) fusion(bf16[96,512]{1,0:T(8,128)(2,1)S(1)} %copy-done.8, f32[96,512]{1,0:T(8,128)} %copy-done.9, f32[96,512]{1,0:T(8,128)S(1)} %copy.105, f32[64,96]{1,0:T(8,128)S(1)} %fusion.36, s32[512]{0:T(512)S(1)} %iota_add_fusion, s32[64]{0:T(128)S(1)} %reduce.1, s32[64]{0:T(128)S(1)} %sub.12), kind=kOutput, calls=%fused_computation.29 | convolution fusion | flops 38584320 | bytes 715264 | tf_op jit(solution)/shard_map/dot_general | solution.py:218
  115.1 0.7 convolution_convert_fusion
  115.8 0.2 convert_element_type.122
  116.0 26.4 %all_to_all.34 = bf16[32,6,1536]{2,1,0:T(8,128)(2,1)S(1)} all-to-all(bf16[32,6,1536]{2,1,0:T(8,128)(2,1)S(1)} %convert_element_type.122), channel_id=1, replica_groups=mesh['seq'=32,'chan'=16] {'seq'}, dimensions={0} | all-to-all | bytes 1179648 | tf_op jit(solution)/shard_map/all_to_all | solution.py:13
  142.6 0.9 broadcast_in_dim.9
  143.5 4.9 %all-to-all-start.3 = ((bf16[32,6,1536]{2,1,0:T(8,128)(2,1)}), bf16[32,6,1536]{2,1,0:T(8,128)(2,1)S(1)}, u32[]{:S(2)}, u32[]{:S(2)}) async-start(bf16[32,6,1536]{2,1,0:T(8,128)(2,1)} %broadcast_in_dim.9), calls=%async_computation.3 | async-start | bytes 1572864 | tf_op jit(solution)/shard_map/all_to_all | solution.py:13
  148.5 0.7 copy.116.scale_ref
  149.6 0.7 copy.115.xdoc_ref
  150.4 0.9 fusion.38
  151.2 19.3 %all-to-all-done.3.in_ref = bf16[32,6,1536]{2,1,0:T(8,128)(2,1)S(1)} async-done(((bf16[32,6,1536]{2,1,0:T(8,128)(2,1)}), bf16[32,6,1536]{2,1,0:T(8,128)(2,1)S(1)}, u32[]{:S(2)}, u32[]{:S(2)}) %all-to-all-start.3) | async-done | bytes 589856 | tf_op jit(solution)/shard_map/all_to_all | solution.py:13
  170.6 0.9 copy-done.1
  171.4 2.2 %shard_map.144 = (f32[96,1536]{1,0:T(8,128)}, f32[96,1536]{1,0:T(8,128)}) custom-call(bf16[32,6,1536]{2,1,0:T(8,128)(2,1)} %copy-done.1), custom_call_target="tpu_custom_call" | custom-call | bytes 1769472 | tf_op jit(solution)/shard_map/pallas_call | solution.py:78
  173.7 1.8 shard_map.145
  (77 shorter events, 3.8 us)
Async XLA Ops:
  7.2 54.0 %copy-start = (bf16[96,1536]{1,0:T(8,128)(2,1)S(1)}, bf16[96,1536]{1,0:T(8,128)(2,1)}, u32[]{:S(2)}) copy-start(bf16[96,1536]{1,0:T(8,128)(2,1)} %param.10) | copy-start | bytes 884740
  7.2 52.9 %copy-start.2 = (bf16[2,256,256]{2,1,0:T(8,128)(2,1)S(1)}, bf16[2,256,256]{2,1,0:T(8,128)(2,1)}, u32[]{:S(2)}) copy-start(bf16[2,256,256]{2,1,0:T(8,128)(2,1)} %param.12) | copy-start | bytes 786436
  7.2 50.9 %all-gather.2.cloned.1.call-start = ((), (), s32[]{:S(2)}) async-start(), calls=%async_computation.5 | async-start | bytes 2088960 | tf_op jit(solution)/shard_map/all_gather | solution.py:109
  58.1 2.4 %copy-start.6 = (bf16[1536,640]{1,0:T(8,128)(2,1)S(1)}, bf16[1536,640]{1,0:T(8,128)(2,1)}, u32[]{:S(2)}) copy-start(bf16[1536,640]{1,0:T(8,128)(2,1)} %all-gather.2.cloned.1.call-done) | copy-start | bytes 5898244
  60.1 1.1 copy-start.8
  61.7 27.6 %copy-start.9 = (f32[96,512]{1,0:T(8,128)}, f32[96,512]{1,0:T(8,128)S(1)}, u32[]{:S(2)}) copy-start(f32[96,512]{1,0:T(8,128)S(1)} %get-tuple-element.34) | copy-start | bytes 589828
  62.5 12.3 %copy-start.5 = (s32[64]{0:T(128)S(1)}, s32[64]{0:T(128)}, u32[]{:S(2)}) copy-start(s32[64]{0:T(128)} %param.16) | copy-start | bytes 772
  65.0 22.9 %all-to-all-start = ((bf16[32,2,2176]{2,1,0:T(2,128)(2,1)}), bf16[32,2,2176]{2,1,0:T(2,128)(2,1)S(1)}, u32[]{:S(2)}, u32[]{:S(2)}) async-start(bf16[32,2,2176]{2,1,0:T(2,128)(2,1)} %reshape.206), calls=%async_computation | async-start | bytes 557056 | tf_op jit(solution)/shard_map/all_to_all | solution.py:13
  74.9 14.0 %copy-start.3 = (bf16[8,64,64]{2,1,0:T(8,128)(2,1)S(1)}, bf16[8,64,64]{2,1,0:T(8,128)(2,1)}, u32[]{:S(2)}) copy-start(bf16[8,64,64]{2,1,0:T(8,128)(2,1)} %param.13) | copy-start | bytes 196612
  88.7 1.5 copy-start.4
  92.1 17.6 %all-to-all-start.1 = ((bf16[32,2,2432]{2,1,0:T(2,128)(2,1)}), bf16[32,2,2432]{2,1,0:T(2,128)(2,1)S(1)}, u32[]{:S(2)}, u32[]{:S(2)}) async-start(bf16[32,2,2432]{2,1,0:T(2,128)(2,1)} %reshape.208), calls=%async_computation.1 | async-start | bytes 622592 | tf_op jit(solution)/shard_map/all_to_all | solution.py:13
  96.7 76.9 %reduce-scatter.2.cloned.1.call-start = ((), (), s32[]{:S(2)}) async-start(), calls=%async_computation.6 | async-start | bytes 1253376 | tf_op jit(solution)/shard_map/reduce_scatter | solution.py:250
  113.0 2.1 %copy-start.7 = (bf16[1536,640]{1,0:T(8,128)(2,1)S(1)}, bf16[1536,640]{1,0:T(8,128)(2,1)}, u32[]{:S(2)}) copy-start(bf16[1536,640]{1,0:T(8,128)(2,1)} %all-gather.2.cloned.1.call-done) | copy-start | bytes 5898244
  143.5 27.0 %all-to-all-start.3 = ((bf16[32,6,1536]{2,1,0:T(8,128)(2,1)}), bf16[32,6,1536]{2,1,0:T(8,128)(2,1)S(1)}, u32[]{:S(2)}, u32[]{:S(2)}) async-start(bf16[32,6,1536]{2,1,0:T(8,128)(2,1)} %broadcast_in_dim.9), calls=%async_computation.3 | async-start | bytes 1572864 | tf_op jit(solution)/shard_map/all_to_all | solution.py:13
  170.6 0.9 copy-start.1
Sparse Core Ops, SparseCore 0:
  10.7 47.3 all-gather.1
  113.2 55.7 reduce-scatter.1

commit v2 on v0

--- a/solution.py
+++ b/solution.py
@@ -11,14 +11,6 @@
 
 def seq_exchange(x):
     return lax.all_to_all(x, "seq", 0, 0, tiled=True)
-
-
-def tiled_exchange(x):
-    n, width = x.shape
-    unit = 8 * 128
-    padded = -(-width // unit) * unit
-    x = jnp.pad(x, ((0, 0), (0, padded - width))).reshape(n, padded // 128, 128)
-    return seq_exchange(x).reshape(n, padded)[:, :width]
 
 
 def split_hi_lo(x):
@@ -144,7 +136,7 @@
         ],
         axis=1,
     )
-    recv2 = tiled_exchange(jnp.concatenate([mix_send, split_hi_lo(small_send)], axis=1))
+    recv2 = seq_exchange(jnp.concatenate([mix_send, split_hi_lo(small_send)], axis=1))
     mix2 = recv2[:, :n_mix].reshape(n_seq, blocks_here, k_here, 2 * chan_rows)
     columns = mix2[..., :chan_rows].reshape(n_seq * blocks_here, k_here, chan_rows)
     d_outer = mix2[..., chan_rows:].reshape(n_seq * blocks_here, k_here, chan_rows)
@@ -183,7 +175,7 @@
     send3 = jnp.concatenate(
         [jnp.concatenate([outer_send, dinner_send], axis=3).reshape(n_seq, -1), piece_b], axis=1
     )
-    recv3_all = tiled_exchange(send3)
+    recv3_all = seq_exchange(send3)
     recv3 = recv3_all[:, :n_mix].reshape(n_seq, blocks_here, k_here, 2 * chan_rows)
     gath3 = join_hi_lo(recv3_all[:, n_mix:])
     outer_tok = (
@@ -233,7 +225,9 @@
         d_second_part.reshape(k_here, n_chan, m_part, n_blk2).transpose(1, 0, 2, 3).reshape(n_chan, -1)
     )
     g_send = jnp.broadcast_to(g_gath, (n_chan, n_doc * lat))
-    fac_send = jnp.concatenate([first_send, second_send, g_send], axis=1)
+    fac_send = jnp.concatenate(
+        [p.reshape(n_chan, -1, 128) for p in (first_send, second_send, g_send)], axis=1
+    )
     fac_red = lax.psum_scatter(fac_send.reshape(-1, 128), "chan", scatter_dimension=0, tiled=True)
     proj_bf = proj_red.astype(jnp.bfloat16)
     gath5 = seq_exchange(jnp.broadcast_to(proj_bf[None], (n_seq, rows_here, width)))

time: 197 us -> 191 us (0.970)
  blocking collectives: 0 us -> 16.5 us
  waiting for transfers between devices: 115 us -> 105 us
  starting transfers between devices: 32.5 us -> 24.4 us
  matrix products: 12.9 us -> 8.64 us
  other arithmetic: 3.41 us -> 6.09 us
    all_to_all x0 -> x1, blocking collectives: none -> 16.5 us  [seq_exchange(): return lax.all_to_all(x, 'seq', 0, 0, tiled=True)]
    all_to_all x4 -> x3, waiting for transfers between devices: 53.2 us -> 42.9 us  [seq_exchange(): return lax.all_to_all(x, 'seq', 0, 0, tiled=True)]
    all_to_all x4 -> x3, starting transfers between devices: 32.4 us -> 24.4 us  [seq_exchange(): return lax.all_to_all(x, 'seq', 0, 0, tiled=True)]
  transfers between devices with their start and end apart: 6 -> 5, of which waited for: 6 -> 5; matrix products, arithmetic and copies ran while one was open for 6% -> 6% of each run, Pallas kernels for 0% -> 0%
where the time goes in v2:
time: 191 us; the launch traced here: 189 us
  waiting for transfers between devices  105 us (55%)
  starting transfers between devices  24.4 us (13%)
  blocking collectives  16.5 us (9%)
  between operations  14.6 us (8%)
  local copies, waits for them, and re-layouts  12.1 us (6%)
  matrix products  8.64 us (5%)
  other arithmetic  6.09 us (3%)
    all_gather x1, waiting for transfers between devices, body(): gathered_all = lax.all_gather(packed, 'chan', axis=0, tiled=True)  47.6 us
    all_to_all x3, waiting for transfers between devices, seq_exchange(): return lax.all_to_all(x, 'seq', 0, 0, tiled=True)  42.9 us
    all_to_all x3, starting transfers between devices, seq_exchange(): return lax.all_to_all(x, 'seq', 0, 0, tiled=True)  24.4 us
    all_to_all x1, blocking collectives, seq_exchange(): return lax.all_to_all(x, 'seq', 0, 0, tiled=True)  16.5 us
    reduce_scatter x1, waiting for transfers between devices, body(): lax.psum_scatter(fac_send.reshape(-1, 128), 'chan', scatter_dimension=0,...  14.4 us
  transfers between devices with their start and end apart: 5, of which 5 were waited for; matrix products, arithmetic and copies ran while one was open for 6% of the time, Pallas kernels for 0%

profile of v2, /device:TPU:1, one launch (start us, length us, event | category | flops | bytes accessed | tf_op | source)
XLA Modules:
  0.0 189.0 jit_solution(17277376500861126666)
XLA Ops:
  7.2 1.6 pad_maximum_fusion.3
  8.9 0.7 copy.92
  9.9 0.7 sub.12
  10.5 1.1 fusion.27
  11.8 47.6 %all-gather.2.cloned.1.call-done = bf16[1536,640]{1,0:T(8,128)(2,1)} async-done(((bf16[96,640]{1,0:T(8,128)(2,1)}), bf16[1536,640]{1,0:T(8,128)(2,1)}) %all-gather.2.cloned.1.call-update) | async-done | bytes 1966096 | tf_op jit(solution)/shard_map/all_gather | solution.py:88
  59.4 2.0 %convolution_convert_fusion.3 = bf16[512,96]{0,1:T(8,128)(2,1)S(1)} fusion(bf16[96,1536]{1,0:T(8,128)(2,1)} %param.11, bf16[1536,640]{1,0:T(8,128)(2,1)} %all-gather.2.cloned.1.call-done), kind=kOutput, calls=%fused_computation.6 | convolution fusion | flops 151044096 | bytes 1966080 | tf_op jit(solution)/shard_map/dot_general | solution.py:101
  61.4 0.2 fusion
  61.8 0.4 fusion.3
  62.2 0.3 fusion.32
  62.5 0.4 fusion.16
  63.3 0.3 reshape.175
  63.5 0.3 fusion.15
  64.1 0.5 broadcast.27
  64.7 0.8 reduce.2
  65.5 0.8 reshape.207
  66.2 9.3 %all-to-all-start = ((bf16[32,2,2176]{2,1,0:T(2,128)(2,1)}), bf16[32,2,2176]{2,1,0:T(2,128)(2,1)S(1)}, u32[]{:S(2)}, u32[]{:S(2)}) async-start(bf16[32,2,2176]{2,1,0:T(2,128)(2,1)} %reshape.207), calls=%async_computation | async-start | bytes 557056 | tf_op jit(solution)/shard_map/all_to_all | solution.py:13
  75.6 10.0 %all-to-all-done = bf16[32,2,2176]{2,1,0:T(2,128)(2,1)S(1)} async-done(((bf16[32,2,2176]{2,1,0:T(2,128)(2,1)}), bf16[32,2,2176]{2,1,0:T(2,128)(2,1)S(1)}, u32[]{:S(2)}, u32[]{:S(2)}) %all-to-all-start) | async-done | bytes 278560 | tf_op jit(solution)/shard_map/all_to_all | solution.py:13
  85.6 0.2 reshape.208
  86.2 0.3 reshape.183
  87.2 0.2 convolution_convert_fusion.2
  87.8 0.3 reshape.188
  88.0 0.2 convolution_bitcast_fusion.1
  88.3 0.8 reduce.3
  89.2 16.5 %all_to_all.34 = bf16[32,2,2432]{2,1,0:T(2,128)(2,1)S(1)} all-to-all(bf16[32,2,2432]{2,1,0:T(2,128)(2,1)S(1)} %reshape.209), channel_id=1, replica_groups=mesh['seq'=32,'chan'=16] {'seq'}, dimensions={0} | all-to-all | bytes 622592 | tf_op jit(solution)/shard_map/all_to_all | solution.py:13
  105.7 0.3 reshape.210
  106.1 0.3 reshape.192
  106.4 0.2 fusion.38
  106.9 0.2 fusion.1
  107.1 1.0 fusion.10
  108.1 0.3 copy-done.6
  108.4 0.7 convolution_convert_fusion
  109.1 1.1 convert_element_type.126
  110.2 6.8 %all-to-all-start.2 = ((bf16[32,6,1536]{2,1,0:T(8,128)(2,1)}), bf16[32,6,1536]{2,1,0:T(8,128)(2,1)S(1)}, u32[]{:S(2)}, u32[]{:S(2)}) async-start(bf16[32,6,1536]{2,1,0:T(8,128)(2,1)} %convert_element_type.126), calls=%async_computation.2 | async-start | bytes 1572864 | tf_op jit(solution)/shard_map/all_to_all | solution.py:13
  117.1 0.2 fusion.39
  117.5 0.2 fusion.17
  117.8 1.1 pad_maximum_fusion
  119.0 16.8 %all-to-all-done.2 = bf16[32,6,1536]{2,1,0:T(8,128)(2,1)S(1)} async-done(((bf16[32,6,1536]{2,1,0:T(8,128)(2,1)}), bf16[32,6,1536]{2,1,0:T(8,128)(2,1)S(1)}, u32[]{:S(2)}, u32[]{:S(2)}) %all-to-all-start.2) | async-done | bytes 589856 | tf_op jit(solution)/shard_map/all_to_all | solution.py:13
  135.9 1.0 broadcast_in_dim.9
  136.9 8.3 %all-to-all-start.3 = ((bf16[32,6,1536]{2,1,0:T(8,128)(2,1)}), bf16[32,6,1536]{2,1,0:T(8,128)(2,1)S(1)}, u32[]{:S(2)}, u32[]{:S(2)}) async-start(bf16[32,6,1536]{2,1,0:T(8,128)(2,1)} %broadcast_in_dim.9), calls=%async_computation.3 | async-start | bytes 1572864 | tf_op jit(solution)/shard_map/all_to_all | solution.py:13
  145.2 0.7 copy.116.scale_ref
  146.3 0.7 copy.115.xdoc_ref
  147.1 0.9 fusion.40
  147.9 16.1 %all-to-all-done.3 = bf16[32,6,1536]{2,1,0:T(8,128)(2,1)S(1)} async-done(((bf16[32,6,1536]{2,1,0:T(8,128)(2,1)}), bf16[32,6,1536]{2,1,0:T(8,128)(2,1)S(1)}, u32[]{:S(2)}, u32[]{:S(2)}) %all-to-all-start.3) | async-done | bytes 589856 | tf_op jit(solution)/shard_map/all_to_all | solution.py:13
  164.0 0.2 fusion.34
  164.2 0.9 slice.114
  165.1 0.9 slice.112
  166.0 14.4 %reduce-scatter.2.cloned.1.call-done.fac_ref = f32[144,128]{1,0:T(8,128)} async-done(((f32[2304,128]{1,0:T(8,128)}), f32[144,128]{1,0:T(8,128)}) %reduce-scatter.2.cloned.1.call-update) | async-done | bytes 73744 | tf_op jit(solution)/shard_map/reduce_scatter | solution.py:231
  180.4 1.8 shard_map.144
  (74 shorter events, 4.0 us)
Async XLA Ops:
  7.2 55.3 %copy-start = (bf16[96,1536]{1,0:T(8,128)(2,1)S(1)}, bf16[96,1536]{1,0:T(8,128)(2,1)}, u32[]{:S(2)}) copy-start(bf16[96,1536]{1,0:T(8,128)(2,1)} %param.10) | copy-start | bytes 884740
  7.2 54.2 %copy-start.1 = (bf16[2,256,256]{2,1,0:T(8,128)(2,1)S(1)}, bf16[2,256,256]{2,1,0:T(8,128)(2,1)}, u32[]{:S(2)}) copy-start(bf16[2,256,256]{2,1,0:T(8,128)(2,1)} %param.12) | copy-start | bytes 786436
  7.2 52.2 %all-gather.2.cloned.1.call-start = ((), (), s32[]{:S(2)}) async-start(), calls=%async_computation.5 | async-start | bytes 2088960 | tf_op jit(solution)/shard_map/all_gather | solution.py:88
  59.4 2.4 %copy-start.5 = (bf16[1536,640]{1,0:T(8,128)(2,1)S(1)}, bf16[1536,640]{1,0:T(8,128)(2,1)}, u32[]{:S(2)}) copy-start(bf16[1536,640]{1,0:T(8,128)(2,1)} %all-gather.2.cloned.1.call-done) | copy-start | bytes 5898244
  61.4 1.1 copy-start.7
  63.8 11.7 %copy-start.4 = (s32[64]{0:T(128)S(1)}, s32[64]{0:T(128)}, u32[]{:S(2)}) copy-start(s32[64]{0:T(128)} %param.16) | copy-start | bytes 772
  66.2 19.4 %all-to-all-start = ((bf16[32,2,2176]{2,1,0:T(2,128)(2,1)}), bf16[32,2,2176]{2,1,0:T(2,128)(2,1)S(1)}, u32[]{:S(2)}, u32[]{:S(2)}) async-start(bf16[32,2,2176]{2,1,0:T(2,128)(2,1)} %reshape.207), calls=%async_computation | async-start | bytes 557056 | tf_op jit(solution)/shard_map/all_to_all | solution.py:13
  75.6 11.1 %copy-start.2 = (bf16[8,64,64]{2,1,0:T(8,128)(2,1)S(1)}, bf16[8,64,64]{2,1,0:T(8,128)(2,1)}, u32[]{:S(2)}) copy-start(bf16[8,64,64]{2,1,0:T(8,128)(2,1)} %param.13) | copy-start | bytes 196612
  86.5 1.5 copy-start.3
  106.9 1.5 copy-start.6
  110.2 25.5 %all-to-all-start.2 = ((bf16[32,6,1536]{2,1,0:T(8,128)(2,1)}), bf16[32,6,1536]{2,1,0:T(8,128)(2,1)S(1)}, u32[]{:S(2)}, u32[]{:S(2)}) async-start(bf16[32,6,1536]{2,1,0:T(8,128)(2,1)} %convert_element_type.126), calls=%async_computation.2 | async-start | bytes 1572864 | tf_op jit(solution)/shard_map/all_to_all | solution.py:13
  117.0 63.4 %reduce-scatter.2.cloned.1.call-start = ((), (), s32[]{:S(2)}) async-start(), calls=%async_computation.6 | async-start | bytes 1253376 | tf_op jit(solution)/shard_map/reduce_scatter | solution.py:231
  136.9 27.1 %all-to-all-start.3 = ((bf16[32,6,1536]{2,1,0:T(8,128)(2,1)}), bf16[32,6,1536]{2,1,0:T(8,128)(2,1)S(1)}, u32[]{:S(2)}, u32[]{:S(2)}) async-start(bf16[32,6,1536]{2,1,0:T(8,128)(2,1)} %broadcast_in_dim.9), calls=%async_computation.3 | async-start | bytes 1572864 | tf_op jit(solution)/shard_map/all_to_all | solution.py:13
Sparse Core Ops, SparseCore 0:
  10.7 48.6 all-gather.1
  120.7 59.6 reduce-scatter.1
